TPU v7x, 256 devices: a whole 4x4x8 slice. The times are simulated.
256 devices in a mesh: seq: 32 (over z, x), head: 8 (over y, core).
Axes of the slice: x: 4, y: 4, z: 8, core: 2. Of those that a mesh axis runs over, the one named last changes fastest.
Arguments:
- queries: bfloat16 [16384, 1024], P(('seq', 'head')), may hold values from -24 to 24
- keys: bfloat16 [16384, 1024], P(('seq', 'head')), may hold values from -6 to 6
- values: bfloat16 [16384, 1024], P(('seq', 'head')), may hold values from -6 to 6
- out_grad: bfloat16 [16384, 1024], P(('seq', 'head')), may hold values from -6 to 6
- key_blocks: int32 [128, 8], replicated, may hold values from 0 to 127, as said below
- counts: int32 [128], replicated, may hold values from 2 to 8, as said below
Outputs:
- attention: bfloat16 [16384, 1024], P('seq', 'head')
- query_grad: bfloat16 [16384, 1024], P('seq', 'head')
- key_grad: bfloat16 [16384, 1024], P('seq', 'head')
- value_grad: bfloat16 [16384, 1024], P('seq', 'head')
Inputs may be any that keep to these rules, and one draw needn't show every extreme that they name: `counts`: some query block uses all 8 listed blocks. `key_blocks`: row a lists 8 different blocks, the first being block a itself and the second block (a - 1) modulo 128; only the first counts[a] of them are used.
All inputs are finite; a program needn't handle non-finite values.
Results may differ from a plain program's by a relative error of at most 0.015.
Values may be sent and summed in bfloat16 or wider, within the bound.
A program may use at most 64 MiB of HBM per device.

v0:
```python
import math
import jax
import jax.numpy as jnp
from jax import lax
from jax.sharding import PartitionSpec as P

HEADS = 8
BLK = 128
neg_fill = -1e30
tile_limit = 512


def block_table(key_blocks, counts):
    block_count = key_blocks.shape[0]
    slot_ids = jnp.arange(key_blocks.shape[1])
    live_slot = slot_ids[None, :] < counts[:, None]
    matches = (key_blocks[:, :, None] == jnp.arange(block_count)[None, None, :]) & live_slot[
        :, :, None
    ]
    return jnp.any(matches, axis=1).astype(jnp.float32)


def one_hot_rows(first_row, row_total, block_count):
    block_ids = (first_row + jnp.arange(row_total)) // BLK
    return (block_ids[:, None] == jnp.arange(block_count)[None, :]).astype(jnp.float32)


def on_device(queries, keys, values, out_grad, key_blocks, counts):
    heads_here = HEADS // lax.axis_size("head")
    q_rows, k_rows, v_rows, g_rows = (
        lax.all_to_all(queries, "head", split_axis=1, concat_axis=0, tiled=True),
        lax.all_to_all(keys, "head", split_axis=1, concat_axis=0, tiled=True),
        lax.all_to_all(values, "head", split_axis=1, concat_axis=0, tiled=True),
        lax.all_to_all(out_grad, "head", split_axis=1, concat_axis=0, tiled=True),
    )
    row_count = q_rows.shape[0]
    feat_width = q_rows.shape[1]
    head_dim = feat_width // heads_here
    score_scale = 1.0 / math.sqrt(head_dim)
    block_count = key_blocks.shape[0]
    slot_total = key_blocks.shape[1]
    local_blocks = row_count // BLK
    first_block = lax.axis_index("seq") * local_blocks
    listed = lax.dynamic_slice_in_dim(key_blocks, first_block, local_blocks, 0)
    used = lax.dynamic_slice_in_dim(counts, first_block, local_blocks, 0)
    slot_ids = jnp.arange(slot_total)
    live = jnp.repeat(slot_ids[None, :] < used[:, None], BLK, axis=1)
    live_mask = live[:, None, None, :]

    def listed_sets(k_whole, v_whole):
        k_blocks = k_whole.reshape(block_count, BLK, heads_here, head_dim)
        v_blocks = v_whole.reshape(block_count, BLK, heads_here, head_dim)
        key_set = jnp.take(k_blocks, listed, axis=0).reshape(
            local_blocks, slot_total * BLK, heads_here, head_dim
        )
        value_set = jnp.take(v_blocks, listed, axis=0).reshape(
            local_blocks, slot_total * BLK, heads_here, head_dim
        )
        return (key_set, value_set)

    q_blocks = q_rows.reshape(local_blocks, BLK, heads_here, head_dim)
    g_blocks = g_rows.reshape(local_blocks, BLK, heads_here, head_dim)

    def block_scores(key_set):
        scores = (
            jnp.einsum("bqhd,bkhd->bhqk", q_blocks, key_set, preferred_element_type=jnp.float32)
            * score_scale
        )
        return jnp.where(live_mask, scores, neg_fill)

    k_whole, v_whole = (
        lax.all_gather(k_rows, "seq", axis=0, tiled=True),
        lax.all_gather(v_rows, "seq", axis=0, tiled=True),
    )
    key_set, value_set = listed_sets(k_whole, v_whole)
    scores = block_scores(key_set)
    row_max = jnp.max(scores, axis=3)
    weights = jnp.where(live_mask, jnp.exp(scores - row_max[..., None]), 0.0)
    row_sum = jnp.sum(weights, axis=3)
    mixed = jnp.einsum(
        "bhqk,bkhd->bqhd",
        weights.astype(jnp.bfloat16),
        value_set,
        preferred_element_type=jnp.float32,
    )
    attention = (mixed / jnp.transpose(row_sum, (0, 2, 1))[..., None]).astype(jnp.bfloat16)
    block_total = row_max + jnp.log(row_sum)
    block_dot = jnp.sum(g_blocks.astype(jnp.float32) * attention.astype(jnp.float32), axis=3)
    dot_bhq = jnp.transpose(block_dot, (0, 2, 1))
    log_total = jnp.transpose(block_total, (0, 2, 1)).reshape(row_count, heads_here)
    grad_dot = block_dot.reshape(row_count, heads_here)
    k_second, v_second = (
        lax.all_gather(k_rows, "seq", axis=0, tiled=True),
        lax.all_gather(v_rows, "seq", axis=0, tiled=True),
    )
    key_again, value_again = listed_sets(k_second, v_second)
    scores_again = block_scores(key_again)
    probs = jnp.where(live_mask, jnp.exp(scores_again - block_total[..., None]), 0.0)
    dprob = jnp.einsum("bqhd,bkhd->bhqk", g_blocks, value_again, preferred_element_type=jnp.float32)
    dscore = (probs * (dprob - dot_bhq[..., None])).astype(jnp.bfloat16)
    query_acc = jnp.einsum("bhqk,bkhd->bqhd", dscore, key_again, preferred_element_type=jnp.float32)
    all_log_total, all_grad_dot = (
        lax.all_gather(log_total, "seq", axis=0, tiled=True),
        lax.all_gather(grad_dot, "seq", axis=0, tiled=True),
    )
    table = block_table(key_blocks, counts)
    local_hot = one_hot_rows(lax.axis_index("seq") * row_count, row_count, block_count)
    key_table = jnp.einsum("bc,kc->bk", table, local_hot)
    k_heads = k_rows.reshape(row_count, heads_here, head_dim)
    v_heads = v_rows.reshape(row_count, heads_here, head_dim)
    zero_heads = jnp.zeros((row_count, heads_here, head_dim), jnp.float32)
    q_piece = lax.all_gather(q_rows, "seq", axis=0, tiled=True)
    g_piece = lax.all_gather(g_rows, "seq", axis=0, tiled=True)
    piece_rows = q_piece.shape[0]
    tile_rows = math.gcd(piece_rows, tile_limit)

    def tile(tile_index, fold_state):
        offset = tile_index * tile_rows
        q_tile = lax.dynamic_slice_in_dim(q_piece, offset, tile_rows, 0).reshape(
            tile_rows, heads_here, head_dim
        )
        g_tile = lax.dynamic_slice_in_dim(g_piece, offset, tile_rows, 0).reshape(
            tile_rows, heads_here, head_dim
        )
        total_tile = lax.dynamic_slice_in_dim(all_log_total, offset, tile_rows, 0)
        dot_tile = lax.dynamic_slice_in_dim(all_grad_dot, offset, tile_rows, 0)
        query_hot = one_hot_rows(offset, tile_rows, block_count)
        allowed = jnp.einsum("qb,bk->qk", query_hot, key_table) > 0.5
        tile_scores = (
            jnp.einsum("qhd,khd->qhk", q_tile, k_heads, preferred_element_type=jnp.float32)
            * score_scale
        )
        tile_scores = jnp.where(allowed[:, None, :], tile_scores, neg_fill)
        tile_probs = jnp.where(
            allowed[:, None, :], jnp.exp(tile_scores - total_tile[:, :, None]), 0.0
        )
        value_acc = fold_state[1] + jnp.einsum(
            "qhk,qhd->khd",
            tile_probs.astype(jnp.bfloat16),
            g_tile,
            preferred_element_type=jnp.float32,
        )
        tile_dprob = jnp.einsum("qhd,khd->qhk", g_tile, v_heads, preferred_element_type=jnp.float32)
        tile_ds = (tile_probs * (tile_dprob - dot_tile[:, :, None])).astype(jnp.bfloat16)
        key_acc = fold_state[0] + jnp.einsum(
            "qhk,qhd->khd", tile_ds, q_tile, preferred_element_type=jnp.float32
        )
        return (key_acc, value_acc)

    key_acc, value_acc = lax.fori_loop(0, piece_rows // tile_rows, tile, (zero_heads, zero_heads))
    query_grad = (query_acc * score_scale).astype(jnp.bfloat16).reshape(row_count, feat_width)
    key_grad = (key_acc * score_scale).astype(jnp.bfloat16).reshape(row_count, feat_width)
    value_grad = value_acc.astype(jnp.bfloat16).reshape(row_count, feat_width)
    return (attention.reshape(row_count, feat_width), query_grad, key_grad, value_grad)


def solution(mesh):
    in_specs = (
        P(("seq", "head"), None),
        P(("seq", "head"), None),
        P(("seq", "head"), None),
        P(("seq", "head"), None),
        P(),
        P(),
    )
    out_specs = (P("seq", "head"), P("seq", "head"), P("seq", "head"), P("seq", "head"))
    return jax.shard_map(
        on_device, mesh=mesh, in_specs=in_specs, out_specs=out_specs, check_vma=False
    )
```

profile of v0, /device:TPU:8, one launch (start us, length us, event | category | flops | bytes accessed | tf_op | source)
XLA Modules:
  0.0 496.2 jit_solution(53246647357267488)
XLA Ops:
  8.1 9.9 %all_to_all.76 = bf16[64,8,128]{2,0,1:T(8,128)(2,1)} all-to-all(bf16[64,8,128]{2,0,1:T(8,128)(2,1)S(1)} %copy_bitcast_fusion.2), channel_id=1, replica_groups=mesh['seq'=32,'head'=8] {'head'}, dimensions={1} | all-to-all | bytes 262144 | tf_op jit(solution)/shard_map/all_to_all | solution.py:32
  19.0 9.2 %all_to_all.77 = bf16[64,8,128]{2,0,1:T(8,128)(2,1)} all-to-all(bf16[64,8,128]{2,0,1:T(8,128)(2,1)S(1)} %copy_bitcast_fusion.3), channel_id=1, replica_groups=mesh['seq'=32,'head'=8] {'head'}, dimensions={1} | all-to-all | bytes 262144 | tf_op jit(solution)/shard_map/all_to_all | solution.py:33
  29.1 9.2 %all_to_all.78 = bf16[64,8,128]{2,0,1:T(8,128)(2,1)} all-to-all(bf16[64,8,128]{2,0,1:T(8,128)(2,1)S(1)} %copy_bitcast_fusion.1), channel_id=1, replica_groups=mesh['seq'=32,'head'=8] {'head'}, dimensions={1} | all-to-all | bytes 262144 | tf_op jit(solution)/shard_map/all_to_all | solution.py:31
  39.3 9.2 %all_to_all.79 = bf16[64,8,128]{2,0,1:T(8,128)(2,1)} all-to-all(bf16[64,8,128]{2,0,1:T(8,128)(2,1)S(1)} %copy_bitcast_fusion), channel_id=1, replica_groups=mesh['seq'=32,'head'=8] {'head'}, dimensions={1} | all-to-all | bytes 262144 | tf_op jit(solution)/shard_map/all_to_all | solution.py:34
  50.0 51.3 %all-gather.7.cloned.1.call-done = bf16[16384,128]{1,0:T(8,128)(2,1)} async-done(((bf16[512,128]{1,0:T(8,128)(2,1)}), bf16[16384,128]{1,0:T(8,128)(2,1)}) %all-gather.7.cloned.1.call-update) | async-done | bytes 4194320 | tf_op jit(solution)/shard_map/all_gather | solution.py:72
  101.3 2.9 gather_fusion.1
  104.3 78.2 %all-gather.5.cloned.1.call-done = bf16[16384,128]{1,0:T(8,128)(2,1)} async-done(((bf16[512,128]{1,0:T(8,128)(2,1)}), bf16[16384,128]{1,0:T(8,128)(2,1)}) %all-gather.5.cloned.1.call-update) | async-done | bytes 4194320 | tf_op jit(solution)/shard_map/all_gather | solution.py:73
  182.5 2.9 gather_fusion
  188.5 47.6 %all_gather.23 = f32[16384,1]{0,1:T(1,128)S(1)} all-gather(f32[512,1]{0,1:T(1,128)S(1)} %bitcast.245), channel_id=1, replica_groups=mesh['seq'=32,'head'=8] {'seq'}, dimensions={0}, use_global_device_ids=true | all-gather | bytes 67584 | tf_op jit(solution)/shard_map/all_gather | solution.py:103
  236.1 2.7 fusion.54
  238.8 47.4 %all_gather.25 = f32[16384,1]{0,1:T(1,128)S(1)} all-gather(f32[512,1]{0,1:T(1,128)S(1)} %bitcast.246), channel_id=1, replica_groups=mesh['seq'=32,'head'=8] {'seq'}, dimensions={0}, use_global_device_ids=true | all-gather | bytes 67584 | tf_op jit(solution)/shard_map/all_gather | solution.py:104
  286.1 3.5 fusion.41
  289.6 55.2 %all-gather.11.cloned.1.call-done = bf16[16384,128]{1,0:T(8,128)(2,1)} async-done(((bf16[512,128]{1,0:T(8,128)(2,1)}), bf16[16384,128]{1,0:T(8,128)(2,1)}) %all-gather.11.cloned.1.call-update) | async-done | bytes 4194320 | tf_op jit(solution)/shard_map/all_gather | solution.py:113
  344.8 143.3 %while.18 = (s32[]{:T(128)}, f32[512,1,128]{0,2,1:T(8,128)S(1)}, f32[512,1,128]{0,2,1:T(8,128)S(1)}, bf16[16384,128]{1,0:T(8,128)(2,1)}, bf16[128,512]{1,0:T(8,1...) while((s32[]{:T(128)}, f32[512,1,128]{0,2,1:T(8,128)S(1)}, ...), condition=%wide.region_5.7_spmd.clone, body=%wide.region_4.6_spmd.clone.sunk | while | flops 338239488 | bytes 5654229 | solution.py:150
  346.6 1.5 fusion.97
  355.5 1.5 fusion.97
  360.0 1.5 fusion.97
  369.0 1.5 fusion.97
  373.5 1.5 fusion.97
  382.4 1.5 fusion.97
  395.8 1.5 fusion.97
  409.3 1.5 fusion.97
  422.7 1.5 fusion.97
  427.2 1.5 fusion.97
  436.1 1.5 fusion.97
  440.6 1.5 fusion.97
  449.6 1.5 fusion.97
  454.0 1.5 fusion.97
  463.0 1.5 fusion.97
  467.5 1.5 fusion.97
  476.4 1.5 fusion.97
  480.9 1.5 fusion.97
  (228 shorter events, 124.0 us)
Async XLA Ops:
  7.2 0.9 copy-start
  7.2 41.3 %copy-start.7 = (s32[128,8]{0,1:T(8,128)S(1)}, s32[128,8]{0,1:T(8,128)}, u32[]{:S(2)}) copy-start(s32[128,8]{0,1:T(8,128)} %param.14) | copy-start | bytes 12292
  7.2 41.8 %copy-start.8 = (s32[128]{0:T(128)S(1)}, s32[128]{0:T(128)}, u32[]{:S(2)}) copy-start(s32[128]{0:T(128)} %param.15) | copy-start | bytes 1540
  7.2 94.1 %all-gather.7.cloned.1.call-start = ((), (), s32[]{:S(2)}) async-start(), calls=%async_computation.5 | async-start | bytes 4325376 | tf_op jit(solution)/shard_map/all_gather | solution.py:72
  18.0 164.5 %all-gather.5.cloned.1.call-start = ((), (), s32[]{:S(2)}) async-start(), calls=%async_computation.4 | async-start | bytes 4325376 | tf_op jit(solution)/shard_map/all_gather | solution.py:73
  28.2 261.5 %all-gather.9.cloned.1.call-start = ((), (), s32[]{:S(2)}) async-start(), calls=%async_computation.6 | async-start | bytes 4325376 | tf_op jit(solution)/shard_map/all_gather | solution.py:112
  38.3 306.5 %all-gather.11.cloned.1.call-start = ((), (), s32[]{:S(2)}) async-start(), calls=%async_computation.7 | async-start | bytes 4325376 | tf_op jit(solution)/shard_map/all_gather | solution.py:113
  185.4 0.9 copy-start.5
  185.7 2.7 copy-start.2
  185.7 50.3 %copy-start.3 = (bf16[4,8,128,1,128]{4,2,1,0,3:T(8,128)(2,1)}, bf16[4,8,128,1,128]{4,2,1,0,3:T(8,128)(2,1)S(1)}, u32[]{:S(2)}) copy-start(bf16[4,8,128,1,128]{4,2,1,0,3:T(8,128)(2,1)S(1)} %get-tuple-element.309) | copy-start | bytes 3145732
  186.3 49.7 %copy-start.6 = (bf16[64,8,128]{2,0,1:T(8,128)(2,1)S(1)}, bf16[64,8,128]{2,0,1:T(8,128)(2,1)}, u32[]{:S(2)}) copy-start(bf16[64,8,128]{2,0,1:T(8,128)(2,1)} %all_to_all.79) | copy-start | bytes 393220
  286.1 58.7 %copy-start.1 = (bf16[64,8,128]{2,0,1:T(8,128)(2,1)S(1)}, bf16[64,8,128]{2,0,1:T(8,128)(2,1)}, u32[]{:S(2)}) copy-start(bf16[64,8,128]{2,0,1:T(8,128)(2,1)} %all_to_all.77) | copy-start | bytes 393220
  286.1 58.7 %copy-start.4 = (bf16[64,8,128]{2,0,1:T(8,128)(2,1)S(1)}, bf16[64,8,128]{2,0,1:T(8,128)(2,1)}, u32[]{:S(2)}) copy-start(bf16[64,8,128]{2,0,1:T(8,128)(2,1)} %all_to_all.76) | copy-start | bytes 393220
Sparse Core Ops, SparseCore 0:
  18.1 83.1 all-gather.6
  103.9 78.5 all-gather.4
  185.1 78.5 all-gather.8
  266.1 78.6 all-gather.10
where the time goes:
time: 498 us; the launch traced here: 496 us
  waiting for transfers between devices  185 us (37%)
  matrix products  148 us (30%)
  blocking collectives  132 us (27%)
  between operations  14 us (3%)
  local copies, waits for them, and re-layouts  11.9 us (2%)
    all_gather x1, waiting for transfers between devices, on_device(): lax.all_gather(v_rows, 'seq', axis=0, tiled=True)  78.2 us
    all_gather x1, waiting for transfers between devices, on_device(): g_piece = lax.all_gather(g_rows, 'seq', axis=0, tiled=True)  55.2 us
    all_gather x1, waiting for transfers between devices, on_device(): lax.all_gather(k_rows, 'seq', axis=0, tiled=True)  51.3 us
    dot_general x32, matrix products, tile(): jnp.einsum('qhk,qhd->khd', tile_ds, q_tile, preferred_element_type=jnp.fl...  47.7 us
    all_gather x1, blocking collectives, on_device(): lax.all_gather(log_total, 'seq', axis=0, tiled=True)  47.6 us
    all_gather x1, blocking collectives, on_device(): lax.all_gather(grad_dot, 'seq', axis=0, tiled=True)  47.4 us
    dot_general x32, matrix products, tile(): jnp.einsum('qhd,khd->qhk', q_tile, k_heads, preferred_element_type=jnp.fl...  43.6 us
    dot_general x32, matrix products, tile(): jnp.einsum('qhk,qhd->khd', tile_probs.astype(jnp.bfloat16), g_tile, prefe...  37.8 us
  transfers between devices with their start and end apart: 4, of which 3 were waited for; matrix products, arithmetic and copies ran while one was open for 4% of the time, Pallas kernels for 0%

commit v1 on v0

--- a/solution.py
+++ b/solution.py
@@ -3,6 +3,7 @@
 import jax.numpy as jnp
 from jax import lax
 from jax.sharding import PartitionSpec as P
+from jax.lax import all_to_all, axis_size
 
 HEADS = 8
 BLK = 128
@@ -68,10 +69,16 @@
         )
         return jnp.where(live_mask, scores, neg_fill)
 
-    k_whole, v_whole = (
-        lax.all_gather(k_rows, "seq", axis=0, tiled=True),
-        lax.all_gather(v_rows, "seq", axis=0, tiled=True),
+    review_quotas_up = lambda load: jnp.concatenate(
+        all_to_all(
+            jnp.stack([load] * axis_size("seq"), axis=0),
+            concat_axis=0,
+            axis_name="seq",
+            split_axis=0,
+        ),
+        axis=0,
     )
+    k_whole, v_whole = (review_quotas_up(k_rows), lax.all_gather(v_rows, "seq", axis=0, tiled=True))
     key_set, value_set = listed_sets(k_whole, v_whole)
     scores = block_scores(key_set)
     row_max = jnp.max(scores, axis=3)

time: 498 us -> 583 us (1.17)
  matrix products: 148 us -> 181 us
  waiting for transfers between devices: 185 us -> 216 us
  starting transfers between devices: 0.16 us -> 11.3 us
  local copies, waits for them, and re-layouts: 11.9 us -> 19.7 us
    all_to_all x0 -> x1, waiting for transfers between devices: none -> 32 us  [on_device(): all_to_all(jnp.stack([load] * axis_size('seq'), axis=0), concat_axis=0, a...]
    all_gather x1, waiting for transfers between devices: 51.3 us -> 79.1 us  [on_device(): lax.all_gather(k_rows, 'seq', axis=0, tiled=True)]
    all_gather x1, waiting for transfers between devices: 78.2 us -> 50.5 us  [on_device(): lax.all_gather(v_rows, 'seq', axis=0, tiled=True)]
    dot_general x32, matrix products: 11.2 us -> 33.8 us  [tile(): allowed = jnp.einsum('qb,bk->qk', query_hot, key_table) > 0.5]
    all_to_all x0 -> x1, starting transfers between devices: none -> 11.2 us  [on_device(): all_to_all(jnp.stack([load] * axis_size('seq'), axis=0), concat_axis=0, a...]
    dot_general x32, matrix products: 43.6 us -> 51.1 us  [tile(): jnp.einsum('qhd,khd->qhk', q_tile, k_heads, preferred_element_type=jnp.fl...]
  transfers between devices with their start and end apart: 4 -> 5, of which waited for: 3 -> 4; matrix products, arithmetic and copies ran while one was open for 4% -> 5% of each run, Pallas kernels for 0% -> 0%
where the time goes in v1:
time: 583 us; the launch traced here: 581 us
  waiting for transfers between devices  216 us (37%)
  matrix products  181 us (31%)
  blocking collectives  132 us (23%)
  local copies, waits for them, and re-layouts  19.7 us (3%)
  between operations  13.9 us (2%)
  starting transfers between devices  11.3 us (2%)
    all_gather x1, waiting for transfers between devices, on_device(): lax.all_gather(k_rows, 'seq', axis=0, tiled=True)  79.1 us
    all_gather x1, waiting for transfers between devices, on_device(): g_piece = lax.all_gather(g_rows, 'seq', axis=0, tiled=True)  53.3 us
    dot_general x32, matrix products, tile(): jnp.einsum('qhd,khd->qhk', q_tile, k_heads, preferred_element_type=jnp.fl...  51.1 us
    all_gather x1, waiting for transfers between devices, on_device(): lax.all_gather(v_rows, 'seq', axis=0, tiled=True)  50.5 us
    all_gather x1, blocking collectives, on_device(): lax.all_gather(log_total, 'seq', axis=0, tiled=True)  47.8 us
    dot_general x32, matrix products, tile(): jnp.einsum('qhk,qhd->khd', tile_ds, q_tile, preferred_element_type=jnp.fl...  47.7 us
    all_gather x1, blocking collectives, on_device(): lax.all_gather(grad_dot, 'seq', axis=0, tiled=True)  47.3 us
    dot_general x32, matrix products, tile(): jnp.einsum('qhk,qhd->khd', tile_probs.astype(jnp.bfloat16), g_tile, prefe...  37.8 us
  transfers between devices with their start and end apart: 5, of which 4 were waited for; matrix products, arithmetic and copies ran while one was open for 5% of the time, Pallas kernels for 0%

profile of v1, /device:TPU:8, one launch (start us, length us, event | category | flops | bytes accessed | tf_op | source)
XLA Modules:
  0.0 580.8 jit_solution(9745322151400641127)
XLA Ops:
  8.1 9.9 %all_to_all.78 = bf16[64,8,128]{2,0,1:T(8,128)(2,1)} all-to-all(bf16[64,8,128]{2,0,1:T(8,128)(2,1)S(1)} %copy_bitcast_fusion.2), channel_id=1, replica_groups=mesh['seq'=32,'head'=8] {'head'}, dimensions={1} | all-to-all | bytes 262144 | tf_op jit(solution)/shard_map/all_to_all | solution.py:33
  19.0 9.2 %all_to_all.79 = bf16[64,8,128]{2,0,1:T(8,128)(2,1)} all-to-all(bf16[64,8,128]{2,0,1:T(8,128)(2,1)S(1)} %copy_bitcast_fusion.3), channel_id=1, replica_groups=mesh['seq'=32,'head'=8] {'head'}, dimensions={1} | all-to-all | bytes 262144 | tf_op jit(solution)/shard_map/all_to_all | solution.py:34
  29.1 9.2 %all_to_all.80 = bf16[64,8,128]{2,0,1:T(8,128)(2,1)} all-to-all(bf16[64,8,128]{2,0,1:T(8,128)(2,1)S(1)} %copy_bitcast_fusion.1), channel_id=1, replica_groups=mesh['seq'=32,'head'=8] {'head'}, dimensions={1} | all-to-all | bytes 262144 | tf_op jit(solution)/shard_map/all_to_all | solution.py:32
  39.3 9.2 %all_to_all.81 = bf16[64,8,128]{2,0,1:T(8,128)(2,1)} all-to-all(bf16[64,8,128]{2,0,1:T(8,128)(2,1)S(1)} %copy_bitcast_fusion), channel_id=1, replica_groups=mesh['seq'=32,'head'=8] {'head'}, dimensions={1} | all-to-all | bytes 262144 | tf_op jit(solution)/shard_map/all_to_all | solution.py:35
  48.4 3.8 stack.5
  52.3 11.2 %all-to-all-start.2 = ((bf16[32,512,128]{2,1,0:T(8,128)(2,1)}), bf16[32,512,128]{2,1,0:T(8,128)(2,1)}, u32[]{:S(2)}, u32[]{:S(2)}) async-start(bf16[32,512,128]{2,1,0:T(8,128)(2,1)} %stack.5), calls=%async_computation.2 | async-start | bytes 8388608 | tf_op jit(solution)/shard_map/all_to_all | solution.py:73
  65.6 79.1 %all-gather.7.cloned.1.call-done = bf16[16384,128]{1,0:T(8,128)(2,1)} async-done(((bf16[512,128]{1,0:T(8,128)(2,1)}), bf16[16384,128]{1,0:T(8,128)(2,1)}) %all-gather.7.cloned.1.call-update) | async-done | bytes 4194320 | tf_op jit(solution)/shard_map/all_gather | solution.py:100
  144.7 2.9 gather_fusion.2
  147.6 32.0 %all-to-all-done.2 = bf16[32,512,128]{2,1,0:T(8,128)(2,1)} async-done(((bf16[32,512,128]{2,1,0:T(8,128)(2,1)}), bf16[32,512,128]{2,1,0:T(8,128)(2,1)}, u32[]{:S(2)}, u32[]{:S(2)}) %all-to-all-start.2) | async-done | bytes 4194336 | tf_op jit(solution)/shard_map/all_to_all | solution.py:73
  179.6 3.9 gather_fusion.1
  183.5 50.5 %all-gather.5.cloned.1.call-done = bf16[16384,128]{1,0:T(8,128)(2,1)} async-done(((bf16[512,128]{1,0:T(8,128)(2,1)}), bf16[16384,128]{1,0:T(8,128)(2,1)}) %all-gather.5.cloned.1.call-update) | async-done | bytes 4194320 | tf_op jit(solution)/shard_map/all_gather | solution.py:81
  234.1 3.8 gather_fusion
  237.9 1.9 broadcast_select_fusion
  242.6 47.8 %all_gather.22 = f32[16384,1]{0,1:T(1,128)S(1)} all-gather(f32[512,1]{0,1:T(1,128)S(1)} %bitcast.233), channel_id=1, replica_groups=mesh['seq'=32,'head'=8] {'seq'}, dimensions={0}, use_global_device_ids=true | all-gather | bytes 67584 | tf_op jit(solution)/shard_map/all_gather | solution.py:110
  290.3 3.6 fusion.56
  293.9 47.3 %all_gather.24 = f32[16384,1]{0,1:T(1,128)S(1)} all-gather(f32[512,1]{0,1:T(1,128)S(1)} %bitcast.234), channel_id=1, replica_groups=mesh['seq'=32,'head'=8] {'seq'}, dimensions={0}, use_global_device_ids=true | all-gather | bytes 67584 | tf_op jit(solution)/shard_map/all_gather | solution.py:111
  341.2 1.8 fusion.69
  343.0 53.3 %all-gather.11.cloned.1.call-done = bf16[16384,128]{1,0:T(8,128)(2,1)} async-done(((bf16[512,128]{1,0:T(8,128)(2,1)}), bf16[16384,128]{1,0:T(8,128)(2,1)}) %all-gather.11.cloned.1.call-update) | async-done | bytes 4194320 | tf_op jit(solution)/shard_map/all_gather | solution.py:120
  396.3 172.4 %while.18 = (s32[]{:T(128)}, f32[512,1,128]{0,2,1:T(8,128)S(1)}, f32[512,1,128]{0,2,1:T(8,128)S(1)}, bf16[16384,128]{1,0:T(8,128)(2,1)}, bf16[128,512]{1,0:T(8,1...) while((s32[]{:T(128)}, f32[512,1,128]{0,2,1:T(8,128)S(1)}, ...), condition=%wide.region_5.7_spmd.clone, body=%wide.region_4.6_spmd.clone.sunk | while | flops 338239488 | bytes 5654229 | solution.py:157
  397.4 1.6 fusion.105
  402.8 1.6 fusion.105
  418.9 1.6 fusion.105
  435.1 1.6 fusion.105
  451.3 1.6 fusion.105
  467.4 1.6 fusion.105
  483.6 1.6 fusion.105
  489.0 1.6 fusion.105
  499.8 1.6 fusion.105
  505.2 1.6 fusion.105
  521.3 1.6 fusion.105
  537.5 1.6 fusion.105
  570.3 3.9 fusion.38
  (231 shorter events, 161.8 us)
Async XLA Ops:
  7.2 0.9 copy-start
  7.2 137.5 %all-gather.7.cloned.1.call-start = ((), (), s32[]{:S(2)}) async-start(), calls=%async_computation.6 | async-start | bytes 4325376 | tf_op jit(solution)/shard_map/all_gather | solution.py:100
  18.0 216.1 %all-gather.5.cloned.1.call-start = ((), (), s32[]{:S(2)}) async-start(), calls=%async_computation.5 | async-start | bytes 4325376 | tf_op jit(solution)/shard_map/all_gather | solution.py:81
  28.2 314.9 %all-gather.9.cloned.1.call-start = ((), (), s32[]{:S(2)}) async-start(), calls=%async_computation.7 | async-start | bytes 4325376 | tf_op jit(solution)/shard_map/all_gather | solution.py:119
  52.3 11.8 %copy-start.7 = (s32[128]{0:T(128)S(1)}, s32[128]{0:T(128)}, u32[]{:S(2)}) copy-start(s32[128]{0:T(128)} %param.15) | copy-start | bytes 1540
  52.3 12.1 %copy-start.6 = (s32[128,8]{0,1:T(8,128)S(1)}, s32[128,8]{0,1:T(8,128)}, u32[]{:S(2)}) copy-start(s32[128,8]{0,1:T(8,128)} %param.14) | copy-start | bytes 12292
  52.3 127.4 %all-to-all-start.2 = ((bf16[32,512,128]{2,1,0:T(8,128)(2,1)}), bf16[32,512,128]{2,1,0:T(8,128)(2,1)}, u32[]{:S(2)}, u32[]{:S(2)}) async-start(bf16[32,512,128]{2,1,0:T(8,128)(2,1)} %stack.5), calls=%async_computation.2 | async-start | bytes 8388608 | tf_op jit(solution)/shard_map/all_to_all | solution.py:73
  63.5 332.9 %all-gather.11.cloned.1.call-start = ((), (), s32[]{:S(2)}) async-start(), calls=%async_computation.8 | async-start | bytes 4325376 | tf_op jit(solution)/shard_map/all_gather | solution.py:120
  237.9 1.9 copy-start.3
  239.8 50.5 %copy-start.4 = (bf16[4,8,128,1,128]{4,2,1,0,3:T(8,128)(2,1)}, bf16[4,8,128,1,128]{4,2,1,0,3:T(8,128)(2,1)S(1)}, u32[]{:S(2)}) copy-start(bf16[4,8,128,1,128]{4,2,1,0,3:T(8,128)(2,1)S(1)} %get-tuple-element.310) | copy-start | bytes 3145732
  239.8 50.5 %copy-start.5 = (bf16[64,8,128]{2,0,1:T(8,128)(2,1)S(1)}, bf16[64,8,128]{2,0,1:T(8,128)(2,1)}, u32[]{:S(2)}) copy-start(bf16[64,8,128]{2,0,1:T(8,128)(2,1)} %all_to_all.81) | copy-start | bytes 393220
  293.9 102.4 %copy-start.1 = (bf16[64,8,128]{2,0,1:T(8,128)(2,1)S(1)}, bf16[64,8,128]{2,0,1:T(8,128)(2,1)}, u32[]{:S(2)}) copy-start(bf16[64,8,128]{2,0,1:T(8,128)(2,1)} %all_to_all.79) | copy-start | bytes 393220
  293.9 102.4 %copy-start.2 = (bf16[64,8,128]{2,0,1:T(8,128)(2,1)S(1)}, bf16[64,8,128]{2,0,1:T(8,128)(2,1)}, u32[]{:S(2)}) copy-start(bf16[64,8,128]{2,0,1:T(8,128)(2,1)} %all_to_all.78) | copy-start | bytes 393220
Sparse Core Ops, SparseCore 0:
  18.1 126.5 all-gather.6
  147.3 86.7 all-gather.4
  236.6 78.5 all-gather.8
  317.7 78.5 all-gather.10
